TPU v7x, 32 devices: a whole 2x2x4 slice. The times are simulated.
32 devices in a mesh: lat: 4 (over z), lon: 8 (over y, x, core).
Axes of the slice: x: 2, y: 2, z: 4, core: 2. Of those that a mesh axis runs over, the one named last changes fastest.
Arguments:
- layer_input: float32 [4, 768, 90, 180], P('lat', 'lon'), may hold values from -6 to 6
- grad_output: float32 [4, 768, 90, 180], P('lat', 'lon'), may hold values from -6 to 6
- first_weight: float32 [2, 8, 96, 96], replicated, may hold values from -0.625 to 0.625
- first_bias: float32 [2, 8, 96], replicated, may hold values from -3 to 3
- second_weight: float32 [2, 8, 96, 96], replicated, may hold values from -0.625 to 0.625
- second_bias: float32 [2, 8, 96], replicated, may hold values from -3 to 3
Outputs:
- grad_input: float32 [4, 768, 90, 180], P('lat', 'lon')
- grad_first_weight: float32 [2, 8, 96, 96], replicated
- grad_first_bias: float32 [2, 8, 96], replicated
- grad_second_weight: float32 [2, 8, 96, 96], replicated
- grad_second_bias: float32 [2, 8, 96], replicated
All inputs are finite; a program needn't handle non-finite values.
Results may differ from a plain program's by a relative error of at most 0.0003.
Values sent between devices are 32-bit elements; how exact they have to be, the bound alone decides.
No kernel may reach another device: no remote copies, remote signals or barrier semaphores. Data moves between devices by JAX's collectives and lax.ppermute only.
A program may use at most 192 MiB of HBM per device.

v0:
```python
import math
import jax
import jax.numpy as jnp
from jax import lax
from jax.sharding import PartitionSpec as P

SHRINK = 0.01
GELU_SCALE = math.sqrt(2.0 / math.pi)
GELU_CUBE = 0.044715
HIGHEST = lax.Precision.HIGHEST


def tables(length, count, limit):
    first = jnp.arange(length, dtype=jnp.int32)[:, None]
    second = jnp.arange(count, dtype=jnp.int32)[None, :]
    angle = 2.0 * math.pi / length * (first * second % length).astype(jnp.float32)
    keeper = (second < limit).astype(jnp.float32) / math.sqrt(length)
    return (jnp.cos(angle) * keeper, jnp.sin(angle) * keeper)


def cotangent_weight(length, count):
    index = jnp.arange(count, dtype=jnp.int32)
    edge = (index == 0) | (2 * index == length)
    return jnp.where(edge, 1.0, 2.0).astype(jnp.float32)


def gelu_slope(value):
    inner = GELU_SCALE * (value + GELU_CUBE * value * value * value)
    tangent = jnp.tanh(inner)
    return 0.5 * (1.0 + tangent) + 0.5 * value * (1.0 - tangent * tangent) * GELU_SCALE * (
        1.0 + 3.0 * GELU_CUBE * value * value
    )


def complex_matrix(weight):
    real_part = weight[0]
    imag_part = weight[1]
    upper = jnp.stack([real_part, imag_part], axis=2)
    lower = jnp.stack([-imag_part, real_part], axis=2)
    return jnp.stack([upper, lower], axis=1)


def forward_mix(left, matrix):
    return jnp.einsum("psbir,bpiqj->qsbjr", left, matrix, precision=HIGHEST)


def back_mix(left, matrix):
    return jnp.einsum("qsbjr,bpiqj->psbir", left, matrix, precision=HIGHEST)


def weight_grad(left, right):
    total = jnp.einsum("psbir,qsbjr->bpiqj", left, right, precision=HIGHEST)
    grad_real = total[:, 0, :, 0, :] + total[:, 1, :, 1, :]
    grad_imag = total[:, 0, :, 1, :] - total[:, 1, :, 0, :]
    return jnp.stack([grad_real, grad_imag])


def bias_view(vector):
    return vector[:, None, :, :, None]


def block_backward(x_both, g_both, first_weight, first_bias, second_weight, second_bias):
    parts, samples, channels, modes = x_both.shape
    blocks = first_weight.shape[1]
    width = first_weight.shape[2]
    shape_five = (parts, samples, blocks, width, modes)
    x_both = x_both.reshape(shape_five)
    g_both = g_both.reshape(shape_five)
    first_matrix = complex_matrix(first_weight)
    second_matrix = complex_matrix(second_weight)
    a_both = forward_mix(x_both, first_matrix) + bias_view(first_bias)
    o_both = jax.nn.gelu(a_both, approximate=True)
    z_both = forward_mix(o_both, second_matrix) + bias_view(second_bias)
    e_both = g_both * jnp.tanh(z_both / SHRINK) ** 2
    grad_w_two = weight_grad(o_both, e_both)
    grad_b_two = jnp.sum(e_both, axis=(1, 4))
    s_both = back_mix(e_both, second_matrix) * gelu_slope(a_both)
    grad_w_one = weight_grad(x_both, s_both)
    grad_b_one = jnp.sum(s_both, axis=(1, 4))
    d_both = back_mix(s_both, first_matrix)
    return (
        d_both.reshape((parts, samples, channels, modes)),
        (grad_w_one, grad_b_one, grad_w_two, grad_b_two),
    )


def on_device(layer_input, grad_output, first_weight, first_bias, second_weight, second_bias):
    lon_count = lax.axis_size("lon")
    samples, local_ch, lat_rows, lon_cols = layer_input.shape
    kept_freqs = lon_cols // 2 + 1
    freq_slots = (lon_cols // 2 + lon_count) // lon_count * lon_count
    lon_cos, lon_sin = tables(lon_cols, freq_slots, kept_freqs)
    factor_row = cotangent_weight(lon_cols, freq_slots)[None, :]
    lon_table = jnp.stack([lon_cos, -lon_sin], axis=1)
    cot_table = jnp.stack([lon_cos * factor_row, -lon_sin * factor_row], axis=1)
    lon_back = jnp.stack([lon_cos.T, -lon_sin.T])
    lat_cos, lat_sin = tables(lat_rows, lat_rows, lat_rows)
    lat_table = jnp.stack(
        [jnp.stack([lat_cos, -lat_sin], axis=1), jnp.stack([lat_sin, lat_cos], axis=1)]
    )
    lat_back = jnp.stack(
        [jnp.stack([lat_cos, lat_sin], axis=1), jnp.stack([-lat_sin, lat_cos], axis=1)]
    )

    def lon_forward(data, table):
        return jnp.einsum("schw,wqk->qsckh", data, table, precision=HIGHEST)

    def lat_forward(data):
        return jnp.einsum("psckh,phqm->qsckm", data, lat_table, precision=HIGHEST)

    x_both = lon_forward(layer_input, lon_table)
    g_both = lon_forward(grad_output, cot_table)
    x_both = lat_forward(x_both)
    g_both = lat_forward(g_both)
    flat_shape = (2, samples, local_ch, freq_slots * lat_rows)
    x_modes, g_modes = (
        lax.all_to_all(x_both.reshape(flat_shape), "lon", split_axis=3, concat_axis=2, tiled=True),
        lax.all_to_all(g_both.reshape(flat_shape), "lon", split_axis=3, concat_axis=2, tiled=True),
    )
    d_stack, partial_grads = block_backward(
        x_modes, g_modes, first_weight, first_bias, second_weight, second_bias
    )
    stacked = lax.all_to_all(d_stack, "lon", split_axis=2, concat_axis=3, tiled=True)
    shape_five = (2, stacked.shape[1], stacked.shape[2], freq_slots, lat_rows)
    grad_input = jnp.einsum(
        "qsckh,qkw->schw",
        jnp.einsum("psckm,pmqh->qsckh", stacked.reshape(shape_five), lat_back, precision=HIGHEST),
        lon_back,
        precision=HIGHEST,
    )
    flat_grads = jnp.concatenate([piece.reshape(-1) for piece in partial_grads])
    share = lax.psum_scatter(flat_grads, "lon", scatter_dimension=0, tiled=True)
    summed = lax.psum(share, "lat")
    whole = lax.all_gather(summed, "lon", axis=0, tiled=True)
    results = []
    offset = 0
    for piece in partial_grads:
        results.append(whole[offset : offset + piece.size].reshape(piece.shape))
        offset = offset + piece.size
    grad_w_one, grad_b_one, grad_w_two, grad_b_two = results
    return (grad_input, grad_w_one, grad_b_one, grad_w_two, grad_b_two)


def solution(mesh):
    placed = (P("lat", "lon", None, None), P("lat", "lon", None, None), P(), P(), P(), P())
    return jax.shard_map(
        on_device,
        mesh=mesh,
        in_specs=placed,
        out_specs=(P("lat", "lon", None, None), P(), P(), P(), P()),
        check_vma=False,
    )
```

profile of v0, /device:TPU:0, one launch (start us, length us, event | category | flops | bytes accessed | tf_op | source)
XLA Modules:
  0.0 626.7 jit_solution(1061869455097390078)
XLA Ops:
  8.1 14.8 %fusion.56 = f32[2,96,96,90]{1,2,3,0:T(8,128)} fusion(f32[1,96,90,180]{1,0,3,2:T(1,128)} %param.7, f32[180,1,96]{2,0,1:T(8,128)S(1)} %get-tuple-element.44, f32[180,1,96]{2,0,1:T(8,128)S(1)} %get-tuple-element.43), kind=kOutput, calls=%fused_computation.52 | convolution fusion | flops 3583215360 | bytes 12994560 | tf_op jit(solution)/shard_map/schw,wqk->qsckh/dot_general | solution.py:106
  23.0 12.4 %copy.98 = f32[2,96,96,90]{3,2,0,1:T(8,128)} copy(f32[2,96,96,90]{1,2,3,0:T(8,128)} %fusion.56) | data formatting | bytes 13271040 | tf_op jit(solution)/shard_map/reshape.2
  36.1 14.5 %fusion.50 = f32[2,1,96,96,90]{3,4,2,0,1:T(8,128)} fusion(f32[2,96,96,90]{3,2,0,1:T(8,128)} %copy.98, f32[1,90,2,90]{1,3,0,2:T(8,128)S(1)} %get-tuple-element.38, f32[1,90,2,90]{1,3,0,2:T(8,128)S(1)} %get-tuple-element.41), kind=kOutput, calls=%fused_computation.49 | convolution fusion | flops 3583213056 | bytes 13400640 | tf_op jit(solution)/shard_map/psckh,phqm->qsckm/dot_general | solution.py:109
  50.6 12.5 %copy.150 = f32[2,1,96,96,90]{2,0,4,3,1:T(2,128)} copy(f32[2,1,96,96,90]{3,4,2,0,1:T(8,128)} %fusion.50) | data formatting | bytes 13271040 | tf_op jit(solution)/shard_map/reshape | solution.py:118
  68.6 14.8 %fusion.59 = f32[2,96,96,90]{1,2,3,0:T(8,128)} fusion(f32[1,96,90,180]{1,0,3,2:T(1,128)} %param.6, f32[180,1,96]{2,0,1:T(8,128)S(1)} %get-tuple-element.48, f32[180,1,96]{2,0,1:T(8,128)S(1)} %get-tuple-element.47), kind=kOutput, calls=%fused_computation.53 | convolution fusion | flops 3583215360 | bytes 12994560 | tf_op jit(solution)/shard_map/schw,wqk->qsckh/dot_general | solution.py:106
  83.4 12.4 %copy.103 = f32[2,96,96,90]{3,2,0,1:T(8,128)} copy(f32[2,96,96,90]{1,2,3,0:T(8,128)} %fusion.59) | data formatting | bytes 13271040 | tf_op jit(solution)/shard_map/reshape.7
  95.9 14.5 %fusion.53 = f32[2,1,96,96,90]{3,4,2,0,1:T(8,128)} fusion(f32[2,96,96,90]{3,2,0,1:T(8,128)} %copy.103, f32[1,90,2,90]{1,3,0,2:T(8,128)S(1)} %get-tuple-element.38, f32[1,90,2,90]{1,3,0,2:T(8,128)S(1)} %get-tuple-element.41), kind=kOutput, calls=%fused_computation.50 | convolution fusion | flops 3583213056 | bytes 13400640 | tf_op jit(solution)/shard_map/psckh,phqm->qsckm/dot_general | solution.py:109
  110.4 12.4 %copy.153 = f32[2,1,96,96,90]{2,0,4,3,1:T(2,128)} copy(f32[2,1,96,96,90]{3,4,2,0,1:T(8,128)} %fusion.53) | data formatting | bytes 13271040 | tf_op jit(solution)/shard_map/reshape | solution.py:117
  122.8 45.2 %all-to-all-done = f32[2,1,96,8640]{2,0,1,3:T(2,128)} async-done(((f32[2,1,96,8640]{2,0,1,3:T(2,128)}), f32[2,1,96,8640]{2,0,1,3:T(2,128)}, u32[]{:S(2)}, u32[]{:S(2)}) %all-to-all-start) | async-done | bytes 6635552 | tf_op jit(solution)/shard_map/all_to_all | solution.py:118
  177.3 13.5 %copy.102 = f32[2,1,96,8,1080]{4,2,0,3,1:T(8,128)} copy(f32[2,1,96,8,1080]{2,0,4,3,1:T(2,128)} %bitcast.29) | data formatting | bytes 13271040 | tf_op jit(solution)/shard_map/all_to_all | solution.py:118
  190.8 81.3 %all-to-all-done.1 = f32[2,1,96,8640]{2,0,1,3:T(2,128)} async-done(((f32[2,1,96,8640]{2,0,1,3:T(2,128)}), f32[2,1,96,8640]{2,0,1,3:T(2,128)}, u32[]{:S(2)}, u32[]{:S(2)}) %all-to-all-start.1) | async-done | bytes 6635552 | tf_op jit(solution)/shard_map/all_to_all | solution.py:117
  272.1 13.5 %copy.107 = f32[2,1,96,8,1080]{4,2,0,3,1:T(8,128)} copy(f32[2,1,96,8,1080]{2,0,4,3,1:T(2,128)} %bitcast.43) | data formatting | bytes 13271040 | tf_op jit(solution)/shard_map/all_to_all | solution.py:117
  285.6 9.7 %fusion.43 = f32[8,2,96,1080,1]{3,2,4,1,0:T(8,128)S(1)} fusion(f32[2,1,96,8,1080]{4,2,0,3,1:T(8,128)} %copy.107, f32[8,1,96,2,96]{2,4,1,3,0:T(8,128)S(1)} %get-tuple-element.36, f32[8,1,96,2,96]{2,4,1,3,0:T(8,128)S(1)} %get-tuple-element.35), kind=kOutput, calls=%fused_computation.44 | convolution fusion | flops 3822354432 | bytes 14450688 | tf_op jit(solution)/shard_map/psbir,bpiqj->qsbjr/dot_general | solution.py:44
  295.4 11.7 %fusion.121 = (f32[2,8,96]{2,0,1:T(2,128)S(1)}, f32[2,1,8,96,1080]{4,3,0,2,1:T(8,128)S(1)}) fusion(f32[2,8,96]{2,0,1:T(2,128)S(1)} %copy.109, f32[2,8,96]{2,0,1:T(2,128)S(1)} %copy.108, f32[8,2,96,1080,1]{3,2,4,1,0:T(8,128)S(1)} %fusion.43, f32[8,1,96,2,96]{2,4,1,3,0:T(8,128)S(1)} %copy-done.5, f32[8,1,96,2,96]{2,4,1,3,0:T(8,128)S(1)} %copy-done.4, ...), kind=kOutput, calls=%fused_computation.153 | convolution fusion | flops 3845577216 | bytes 21104640 | tf_op jit(solution)/shard_map/psbir,bpiqj->qsbjr/dot_general | solution.py:44
  309.9 12.7 %fusion.31 = f32[8,2,96,2,96]{4,2,3,1,0:T(8,128)} fusion(f32[2,1,8,96,1080]{4,3,0,2,1:T(8,128)S(1)} %get-tuple-element.53, f32[8,2,96,1080,1]{3,2,4,1,0:T(8,128)S(1)} %fusion.43, f32[2,8,96]{2,0,1:T(2,128)S(1)} %copy.108), kind=kOutput, calls=%fused_computation.32 | convolution fusion | flops 3836989440 | bytes 14456832 | tf_op jit(solution)/shard_map/psbir,qsbjr->bpiqj/dot_general | solution.py:52
  322.6 15.4 %fusion.122 = (f32[2,8,96]{2,0,1:T(2,128)S(1)}, f32[2,1,8,96,1080]{4,3,0,2,1:T(8,128)S(1)}) fusion(f32[2,8,96]{2,0,1:T(2,128)S(1)} %copy.108, f32[8,2,96,1080,1]{3,2,4,1,0:T(8,128)S(1)} %fusion.43, f32[2,1,8,96,1080]{4,3,0,2,1:T(8,128)} %copy-done.13, f32[8,1,96,2,96]{2,4,1,3,0:T(8,128)} %get-tuple-element.34, f32[8,1,96,2,96]{2,4,1,3,0:T(8,128)S(1)} %copy-done.4), kind=kOutput, calls=%fused_computation.154 | convolution fusion | flops 3855530496 | bytes 21098496 | tf_op jit(solution)/shard_map/qsbjr,bpiqj->psbir/dot_general | solution.py:48
  355.4 56.3 %all-reduce.6.cloned.1.call-done = f32[297984]{0:T(1024)} async-done(((f32[297984]{0:T(1024)}), f32[297984]{0:T(1024)}) %all-reduce.6.cloned.1.call-update) | async-done | bytes 1191952
  413.5 35.1 %all-reduce.4.cloned.1.call-done = f32[37248]{0:T(1024)} async-done(((f32[37248]{0:T(1024)}), f32[37248]{0:T(1024)}) %all-reduce.4.cloned.1.call-update) | async-done | bytes 149008 | tf_op jit(solution)/shard_map/psum | solution.py:133
  450.3 9.9 %fusion.47 = f32[2,1,8,96,1080]{4,3,0,2,1:T(8,128)S(1)} fusion(f32[2,1,8,96,1080]{4,3,0,2,1:T(8,128)} %copy-done, f32[8,1,96,2,96]{2,4,1,3,0:T(8,128)S(1)} %get-tuple-element.36, f32[8,1,96,2,96]{2,4,1,3,0:T(8,128)S(1)} %get-tuple-element.35), kind=kOutput, calls=%fused_computation.48 | convolution fusion | flops 3822354432 | bytes 14450688 | tf_op jit(solution)/shard_map/qsbjr,bpiqj->psbir/dot_general | solution.py:48
  463.6 11.4 %copy.113 = f32[2,1,768,1080]{3,0,1,2:T(2,128)} copy(f32[2,1,768,1080]{3,2,0,1:T(8,128)} %bitcast.261) | data formatting | bytes 13271040 | tf_op jit(solution)/shard_map/reshape | solution.py:82
  486.3 74.0 %all-to-all-done.2 = f32[2,1,768,1080]{3,0,1,2:T(2,128)} async-done(((f32[2,1,768,1080]{3,0,1,2:T(2,128)}), f32[2,1,768,1080]{3,0,1,2:T(2,128)}, u32[]{:S(2)}, u32[]{:S(2)}) %all-to-all-start.2) | async-done | bytes 6635552 | tf_op jit(solution)/shard_map/all_to_all | solution.py:123
  570.8 10.7 %reshape.678 = f32[2,96,96,90,1]{3,2,0,1,4:T(8,128)} reshape(f32[2,1,96,8,1080]{4,3,0,2,1:T(8,128)} %copy.156) | data formatting | bytes 13271040 | tf_op jit(solution)/shard_map/reshape.40
  581.5 13.5 %convolution_bitcast_fusion = f32[2,96,96,90]{2,3,1,0:T(8,128)S(1)} fusion(f32[2,96,96,90,1]{3,2,0,1,4:T(8,128)} %reshape.678, f32[1,90,2,90]{1,3,2,0:T(8,128)S(1)} %copy-done.7, f32[1,90,2,90]{1,3,2,0:T(8,128)S(1)} %copy-done.6), kind=kOutput, calls=%fused_computation.51 | convolution fusion | flops 3583213056 | bytes 13400640 | tf_op jit(solution)/shard_map/psckm,pmqh->qsckh/dot_general | solution.py:127
  594.9 15.3 %fusion.62 = f32[1,96,90,180]{1,3,2,0:T(8,128)S(1)} fusion(f32[2,96,96,90]{2,3,1,0:T(8,128)S(1)} %convolution_bitcast_fusion, f32[1,96,180]{1,2,0:T(8,128)S(1)} %get-tuple-element.46, f32[1,96,180]{1,2,0:T(8,128)S(1)} %get-tuple-element.45), kind=kOutput, calls=%fused_computation.54 | convolution fusion | flops 3583215360 | bytes 12994560 | tf_op jit(solution)/shard_map/qsckh,qkw->schw/dot_general | solution.py:125
  (88 shorter events, 74.1 us)
Async XLA Ops:
  7.2 0.5 copy-start.10
  63.1 104.9 %all-to-all-start = ((f32[2,1,96,8640]{2,0,1,3:T(2,128)}), f32[2,1,96,8640]{2,0,1,3:T(2,128)}, u32[]{:S(2)}, u32[]{:S(2)}) async-start(f32[2,1,96,8640]{2,0,1,3:T(2,128)} %bitcast.260), calls=%async_computation | async-start | bytes 17694720 | tf_op jit(solution)/shard_map/all_to_all | solution.py:118
  168.0 5.7 copy-start.8
  168.0 5.7 copy-start.9
  168.0 5.7 copy-start.3
  168.0 104.1 %all-to-all-start.1 = ((f32[2,1,96,8640]{2,0,1,3:T(2,128)}), f32[2,1,96,8640]{2,0,1,3:T(2,128)}, u32[]{:S(2)}, u32[]{:S(2)}) async-start(f32[2,1,96,8640]{2,0,1,3:T(2,128)} %bitcast.259), calls=%async_computation.1 | async-start | bytes 17694720 | tf_op jit(solution)/shard_map/all_to_all | solution.py:117
  173.1 238.6 %all-reduce.6.cloned.1.call-start = ((), (), s32[]{:S(2)}) async-start(), calls=%async_computation.5 | async-start | bytes 2383872
  285.6 9.8 %copy-start.1 = (f32[2,1,96,8,1080]{4,2,0,3,1:T(8,128)S(1)}, f32[2,1,96,8,1080]{4,2,0,3,1:T(8,128)}, u32[]{:S(2)}) copy-start(f32[2,1,96,8,1080]{4,2,0,3,1:T(8,128)} %copy.102) | copy-start | bytes 19906564
  285.6 9.8 %copy-start.4 = (f32[8,1,96,2,96]{2,4,1,3,0:T(8,128)S(1)}, f32[8,1,96,2,96]{2,4,1,3,0:T(8,128)}, u32[]{:S(2)}) copy-start(f32[8,1,96,2,96]{2,4,1,3,0:T(8,128)} %get-tuple-element.33) | copy-start | bytes 1769476
  285.6 9.8 %copy-start.5 = (f32[8,1,96,2,96]{2,4,1,3,0:T(8,128)S(1)}, f32[8,1,96,2,96]{2,4,1,3,0:T(8,128)}, u32[]{:S(2)}) copy-start(f32[8,1,96,2,96]{2,4,1,3,0:T(8,128)} %get-tuple-element.34) | copy-start | bytes 1769476
  307.1 2.9 copy-start.13
  309.9 28.1 %slice-start = ((s8[7077888]{0:T(1024)(128)(4,1)}), s8[4194304]{0:T(1024)(128)(4,1)S(1)}, s32[]{:S(2)}) async-start(s8[7077888]{0:T(1024)(128)(4,1)} %bitcast.257), calls=%async_computation.6 | async-start | bytes 8388608
  322.6 15.5 %slice-start.1 = ((s8[7077888]{0:T(1024)(128)(4,1)}), s8[2883584]{0:T(1024)(128)(4,1)S(1)}, s32[]{:S(2)}) async-start(s8[7077888]{0:T(1024)(128)(4,1)} %bitcast.257), calls=%async_computation.7 | async-start | bytes 5767168
  338.0 8.7 %copy-start = (f32[2,1,8,96,1080]{4,3,0,2,1:T(8,128)}, f32[2,1,8,96,1080]{4,3,0,2,1:T(8,128)S(1)}, u32[]{:S(2)}) copy-start(f32[2,1,8,96,1080]{4,3,0,2,1:T(8,128)S(1)} %get-tuple-element.55) | copy-start | bytes 19906564
  338.1 9.5 %copy-start.2 = (f32[8,2,96,2,96]{4,2,3,1,0:T(8,128)S(1)}, f32[8,2,96,2,96]{4,2,3,1,0:T(8,128)}, u32[]{:S(2)}) copy-start(f32[8,2,96,2,96]{4,2,3,1,0:T(8,128)} %fusion.31) | copy-start | bytes 3538948
  346.7 7.4 %copy-start.12 = (u32[32]{0:T(128)S(1)}, u32[32]{0:T(128)}, u32[]{:S(2)}) copy-start(u32[32]{0:T(128)} %constant.64) | copy-start | bytes 388
  354.1 94.5 %all-reduce.4.cloned.1.call-start = ((), (), s32[]{:S(2)}) async-start(), calls=%async_computation.3 | async-start | bytes 303104 | tf_op jit(solution)/shard_map/psum | solution.py:133
  413.4 67.3 %all-gather.3.cloned.1.call-start = ((), (), s32[]{:S(2)}) async-start(), calls=%async_computation.4 | async-start | bytes 1340928 | tf_op jit(solution)/shard_map/all_gather | solution.py:134
  475.0 5.2 copy-start.11
  475.0 85.2 %all-to-all-start.2 = ((f32[2,1,768,1080]{3,0,1,2:T(2,128)}), f32[2,1,768,1080]{3,0,1,2:T(2,128)}, u32[]{:S(2)}, u32[]{:S(2)}) async-start(f32[2,1,768,1080]{3,0,1,2:T(2,128)} %copy.113), calls=%async_computation.2 | async-start | bytes 14155776 | tf_op jit(solution)/shard_map/all_to_all | solution.py:123
  570.8 10.7 %copy-start.6 = (f32[1,90,2,90]{1,3,2,0:T(8,128)S(1)}, f32[1,90,2,90]{1,3,2,0:T(8,128)}, u32[]{:S(2)}) copy-start(f32[1,90,2,90]{1,3,2,0:T(8,128)} %get-tuple-element.37) | copy-start | bytes 194404
  570.8 10.7 %copy-start.7 = (f32[1,90,2,90]{1,3,2,0:T(8,128)S(1)}, f32[1,90,2,90]{1,3,2,0:T(8,128)}, u32[]{:S(2)}) copy-start(f32[1,90,2,90]{1,3,2,0:T(8,128)} %get-tuple-element.42) | copy-start | bytes 194404
Sparse Core Ops, SparseCore 0:
  354.2 57.4 all-reduce.5
  414.7 33.8 all-reduce.3
  451.0 24.1 all-gather.2
where the time goes:
time: 637 us; the launch traced here: 627 us
  waiting for transfers between devices  292 us (46%)
  matrix products  156 us (24%)
  local copies, waits for them, and re-layouts  139 us (22%)
  starting transfers between devices  16.4 us (3%)
  between operations  15 us (2%)
  other arithmetic  8.95 us (1%)
    all_to_all x1, waiting for transfers between devices, on_device(): lax.all_to_all(x_both.reshape(flat_shape), 'lon', split_axis=3, concat_ax...  81.3 us
    all_to_all x1, waiting for transfers between devices, on_device(): lax.all_to_all(d_stack, 'lon', split_axis=2, concat_axis=3, tiled=True)  74 us
    unnamed x4, waiting for transfers between devices  56.4 us
    all_to_all x1, waiting for transfers between devices, on_device(): lax.all_to_all(g_both.reshape(flat_shape), 'lon', split_axis=3, concat_ax...  45.2 us
    another operation x4, local copies, waits for them, and re-layouts  42.5 us
    psum x1, waiting for transfers between devices, on_device(): summed = lax.psum(share, 'lat')  35.1 us
    dot_general x2, matrix products, lon_forward(): return jnp.einsum('schw,wqk->qsckh', data, table, precision=HIGHEST)  29.7 us
    dot_general x2, matrix products, lat_forward(): return jnp.einsum('psckh,phqm->qsckm', data, lat_table, precision=HIGHEST)  29.1 us
  transfers between devices with their start and end apart: 6, of which 5 were waited for; matrix products, arithmetic and copies ran while one was open for 16% of the time, Pallas kernels for 0%

commit v1 on v0

--- a/solution.py
+++ b/solution.py
@@ -8,6 +8,27 @@
 GELU_SCALE = math.sqrt(2.0 / math.pi)
 GELU_CUBE = 0.044715
 HIGHEST = lax.Precision.HIGHEST
+
+
+def build_the_streams(q_in, along_axis):
+    high = lax.axis_size(along_axis)
+    part_next, before = (high, lax.axis_index(along_axis))
+    part_now = list(q_in.shape)
+    z = q_in.shape[3] // part_next
+    part_now[3] = z
+    current_block = part_now[2]
+    part_now[2] = current_block * part_next
+    no = 0
+    shaped = jnp.zeros(part_now, q_in.dtype)
+    while no < part_next:
+        b_now = lax.dynamic_slice_in_dim(q_in, (before ^ no) * z, z, axis=3)
+        if no:
+            b_now = lax.ppermute(b_now, along_axis, [(k0, k0 ^ no) for k0 in range(part_next)])
+        shaped = lax.dynamic_update_slice_in_dim(
+            shaped, b_now, (before ^ no) * current_block, axis=2
+        )
+        no = no + 1
+    return shaped
 
 
 def tables(length, count, limit):
@@ -115,7 +136,7 @@
     flat_shape = (2, samples, local_ch, freq_slots * lat_rows)
     x_modes, g_modes = (
         lax.all_to_all(x_both.reshape(flat_shape), "lon", split_axis=3, concat_axis=2, tiled=True),
-        lax.all_to_all(g_both.reshape(flat_shape), "lon", split_axis=3, concat_axis=2, tiled=True),
+        build_the_streams(g_both.reshape(flat_shape), "lon"),
     )
     d_stack, partial_grads = block_backward(
         x_modes, g_modes, first_weight, first_bias, second_weight, second_bias

time: 637 us -> 605 us (0.950)
  waiting for transfers between devices: 292 us -> 245 us
  local copies, waits for them, and re-layouts: 139 us -> 153 us
    all_to_all x1, waiting for transfers between devices: 81.3 us -> 0.01 us  [on_device(): lax.all_to_all(x_both.reshape(flat_shape), 'lon', split_axis=3, concat_ax...]
    ppermute x0 -> x7, waiting for transfers between devices: none -> 79 us  [build_the_streams(): lax.ppermute(b_now, along_axis, [(k0, k0 ^ no) for k0 in range(part_next)])]
    all_to_all x1 -> x0, waiting for transfers between devices: 45.2 us -> none  [on_device(): lax.all_to_all(g_both.reshape(flat_shape), 'lon', split_axis=3, concat_ax...]
    all_to_all x1 -> x0, local copies, waits for them, and re-layouts: 13.5 us -> none  [on_device(): lax.all_to_all(g_both.reshape(flat_shape), 'lon', split_axis=3, concat_ax...]
    dynamic_update_slice x0 -> x7, local copies, waits for them, and re-layouts: none -> 12.9 us  [build_the_streams(): lax.dynamic_update_slice_in_dim(shaped, b_now, (before ^ no) * current_bl...]
    transpose x0 -> x1, local copies, waits for them, and re-layouts: none -> 9.74 us  [lat_forward(): return jnp.einsum('psckh,phqm->qsckm', data, lat_table, precision=HIGHEST)]
    ppermute x0 -> x7, starting transfers between devices: none -> 7.22 us  [build_the_streams(): lax.ppermute(b_now, along_axis, [(k0, k0 ^ no) for k0 in range(part_next)])]
    unnamed x42 -> x46, local copies, waits for them, and re-layouts: 17.5 us -> 20.7 us
  transfers between devices with their start and end apart: 6 -> 12, of which waited for: 5 -> 7; matrix products, arithmetic and copies ran while one was open for 16% -> 19% of each run, Pallas kernels for 0% -> 0%
where the time goes in v1:
time: 605 us; the launch traced here: 595 us
  waiting for transfers between devices  245 us (40%)
  matrix products  156 us (26%)
  local copies, waits for them, and re-layouts  153 us (25%)
  starting transfers between devices  17.8 us (3%)
  between operations  15.4 us (3%)
  other arithmetic  7.32 us (1%)
    ppermute x7, waiting for transfers between devices, build_the_streams(): lax.ppermute(b_now, along_axis, [(k0, k0 ^ no) for k0 in range(part_next)])  79 us
    all_to_all x1, waiting for transfers between devices, on_device(): lax.all_to_all(d_stack, 'lon', split_axis=2, concat_axis=3, tiled=True)  74 us
    unnamed x4, waiting for transfers between devices  56.7 us
    another operation x4, local copies, waits for them, and re-layouts  42.5 us
    psum x1, waiting for transfers between devices, on_device(): summed = lax.psum(share, 'lat')  35.1 us
    dot_general x2, matrix products, lon_forward(): return jnp.einsum('schw,wqk->qsckh', data, table, precision=HIGHEST)  29.7 us
    dot_general x2, matrix products, lat_forward(): return jnp.einsum('psckh,phqm->qsckm', data, lat_table, precision=HIGHEST)  29 us
    dot_general x2, matrix products, back_mix(): return jnp.einsum('qsbjr,bpiqj->psbir', left, matrix, precision=HIGHEST)  25.7 us
  transfers between devices with their start and end apart: 12, of which 7 were waited for; matrix products, arithmetic and copies ran while one was open for 19% of the time, Pallas kernels for 0%

profile of v1, /device:TPU:0, one launch (start us, length us, event | category | flops | bytes accessed | tf_op | source)
XLA Modules:
  0.0 594.8 jit_solution(5855833131593109562)
XLA Ops:
  8.1 14.9 %fusion.57 = f32[2,96,96,90]{1,2,3,0:T(8,128)} fusion(f32[1,96,90,180]{1,0,3,2:T(1,128)} %param.6, f32[180,1,96]{2,0,1:T(8,128)S(1)} %get-tuple-element.56, f32[180,1,96]{2,0,1:T(8,128)S(1)} %get-tuple-element.55), kind=kOutput, calls=%fused_computation.53 | convolution fusion | flops 3583215360 | bytes 12994560 | tf_op jit(solution)/shard_map/schw,wqk->qsckh/dot_general | solution.py:127
  23.0 12.4 %copy.98 = f32[2,96,96,90]{3,2,0,1:T(8,128)} copy(f32[2,96,96,90]{1,2,3,0:T(8,128)} %fusion.57) | data formatting | bytes 13271040 | tf_op jit(solution)/shard_map/reshape.6
  36.1 14.5 %fusion.51 = f32[2,1,96,96,90]{3,4,2,0,1:T(8,128)} fusion(f32[2,96,96,90]{3,2,0,1:T(8,128)} %copy.98, f32[1,90,2,90]{1,3,0,2:T(8,128)S(1)} %get-tuple-element.46, f32[1,90,2,90]{1,3,0,2:T(8,128)S(1)} %get-tuple-element.49), kind=kOutput, calls=%fused_computation.50 | convolution fusion | flops 3583213056 | bytes 13400640 | tf_op jit(solution)/shard_map/psckh,phqm->qsckm/dot_general | solution.py:130
  50.6 13.0 %copy.146 = f32[2,1,96,96,90]{2,0,4,3,1:T(2,128)} copy(f32[2,1,96,96,90]{3,4,2,0,1:T(8,128)} %fusion.51) | data formatting | bytes 13271040 | tf_op jit(solution)/shard_map/reshape | solution.py:138
  69.1 14.9 %fusion.54 = f32[2,96,96,90]{1,2,3,0:T(8,128)} fusion(f32[1,96,90,180]{1,0,3,2:T(1,128)} %param.7, f32[180,1,96]{2,0,1:T(8,128)S(1)} %get-tuple-element.52, f32[180,1,96]{2,0,1:T(8,128)S(1)} %get-tuple-element.51), kind=kOutput, calls=%fused_computation.52 | convolution fusion | flops 3583215360 | bytes 12994560 | tf_op jit(solution)/shard_map/schw,wqk->qsckh/dot_general | solution.py:127
  83.9 12.4 %copy.96 = f32[2,96,96,90]{3,2,0,1:T(8,128)} copy(f32[2,96,96,90]{1,2,3,0:T(8,128)} %fusion.54) | data formatting | bytes 13271040 | tf_op jit(solution)/shard_map/reshape.2
  96.3 14.5 %fusion.48 = f32[2,1,96,96,90]{3,4,2,0,1:T(8,128)} fusion(f32[2,96,96,90]{3,2,0,1:T(8,128)} %copy.96, f32[1,90,2,90]{1,3,0,2:T(8,128)S(1)} %get-tuple-element.46, f32[1,90,2,90]{1,3,0,2:T(8,128)S(1)} %get-tuple-element.49), kind=kOutput, calls=%fused_computation.49 | convolution fusion | flops 3583213056 | bytes 13400640 | tf_op jit(solution)/shard_map/psckh,phqm->qsckm/dot_general | solution.py:130
  120.6 10.2 %reshape.640 = f32[2,1,96,8640]{3,2,0,1:T(8,128)} reshape(f32[2,1,96,96,90]{4,3,2,0,1:T(8,128)} %copy.97) | data formatting | bytes 13271040 | tf_op jit(solution)/shard_map/reshape | solution.py:139
  154.5 32.5 %collective-permute-done.1 = f32[2,1,96,1080]{3,2,0,1:T(8,128)} collective-permute-done((f32[2,1,96,1080]{3,2,0,1:T(8,128)}, f32[2,1,96,1080]{3,2,0,1:T(8,128)}, u32[]{:S(2)}, u32[]{:S(2)}) %collective-permute-start.1) | collective-permute-done | bytes 829472 | tf_op jit(solution)/shard_map/ppermute | solution.py:26
  189.3 15.3 %collective-permute-done.2 = f32[2,1,96,1080]{3,2,0,1:T(8,128)} collective-permute-done((f32[2,1,96,1080]{3,2,0,1:T(8,128)}, f32[2,1,96,1080]{3,2,0,1:T(8,128)}, u32[]{:S(2)}, u32[]{:S(2)}) %collective-permute-start.2) | collective-permute-done | bytes 829472 | tf_op jit(solution)/shard_map/ppermute | solution.py:26
  211.0 14.8 %collective-permute-done.5 = f32[2,1,96,1080]{3,2,0,1:T(8,128)S(1)} collective-permute-done((f32[2,1,96,1080]{3,2,0,1:T(8,128)}, f32[2,1,96,1080]{3,2,0,1:T(8,128)S(1)}, u32[]{:S(2)}, u32[]{:S(2)}) %collective-permute-start.5) | collective-permute-done | bytes 829472 | tf_op jit(solution)/shard_map/ppermute | solution.py:26
  226.9 16.3 %collective-permute-done.6 = f32[2,1,96,1080]{3,2,0,1:T(8,128)S(1)} collective-permute-done((f32[2,1,96,1080]{3,2,0,1:T(8,128)}, f32[2,1,96,1080]{3,2,0,1:T(8,128)S(1)}, u32[]{:S(2)}, u32[]{:S(2)}) %collective-permute-start.6) | collective-permute-done | bytes 829472 | tf_op jit(solution)/shard_map/ppermute | solution.py:26
  244.2 13.5 %copy.102 = f32[2,1,96,8,1080]{4,2,0,3,1:T(8,128)} copy(f32[2,1,96,8,1080]{2,0,4,3,1:T(2,128)} %bitcast.41) | data formatting | bytes 13271040 | tf_op jit(solution)/shard_map/all_to_all | solution.py:138
  267.4 13.1 %fusion.121 = (f32[2,8,96]{2,0,1:T(2,128)}, f32[2,1,8,96,1080]{4,3,0,2,1:T(8,128)}) fusion(f32[2,8,96]{2,0,1:T(2,128)S(1)} %copy.104, f32[2,8,96]{2,0,1:T(2,128)S(1)} %copy.103, f32[8,2,96,1080,1]{3,2,4,1,0:T(8,128)S(1)} %fusion.41, f32[8,1,96,2,96]{2,4,1,3,0:T(8,128)S(1)} %copy-done.6, f32[8,1,96,2,96]{2,4,1,3,0:T(8,128)S(1)} %get-tuple-element.41, ...), kind=kOutput, calls=%fused_computation.168 | convolution fusion | flops 3845577216 | bytes 21104640 | tf_op jit(solution)/shard_map/psbir,bpiqj->qsbjr/dot_general | solution.py:65
  280.6 15.6 %fusion.122 = (f32[2,8,96]{2,0,1:T(2,128)}, f32[2,1,8,96,1080]{4,3,0,2,1:T(8,128)S(1)}) fusion(f32[2,8,96]{2,0,1:T(2,128)S(1)} %copy.103, f32[8,2,96,1080,1]{3,2,4,1,0:T(8,128)S(1)} %fusion.41, f32[2,1,8,96,1080]{4,3,0,2,1:T(8,128)} %get-tuple-element.61, f32[8,1,96,2,96]{2,4,1,3,0:T(8,128)} %get-tuple-element.42, ...), kind=kOutput, calls=%fused_computation.169 | convolution fusion | flops 3855530496 | bytes 21098496 | tf_op jit(solution)/shard_map/qsbjr,bpiqj->psbir/dot_general | solution.py:69
  304.9 11.7 %fusion.31 = f32[8,2,96,2,96]{4,2,3,1,0:T(8,128)S(1)} fusion(f32[2,1,8,96,1080]{4,3,0,2,1:T(8,128)S(1)} %copy-done.15, f32[8,2,96,1080,1]{3,2,4,1,0:T(8,128)S(1)} %fusion.41, f32[2,8,96]{2,0,1:T(2,128)S(1)} %copy.103), kind=kOutput, calls=%fused_computation.32 | convolution fusion | flops 3836989440 | bytes 14456832 | tf_op jit(solution)/shard_map/psbir,qsbjr->bpiqj/dot_general | solution.py:73
  322.9 56.7 %all-reduce.6.cloned.1.call-done = f32[297984]{0:T(1024)} async-done(((f32[297984]{0:T(1024)}), f32[297984]{0:T(1024)}) %all-reduce.6.cloned.1.call-update) | async-done | bytes 1191952
  381.3 35.1 %all-reduce.4.cloned.1.call-done = f32[37248]{0:T(1024)} async-done(((f32[37248]{0:T(1024)}), f32[37248]{0:T(1024)}) %all-reduce.4.cloned.1.call-update) | async-done | bytes 149008 | tf_op jit(solution)/shard_map/psum | solution.py:154
  418.1 10.1 %fusion.45 = f32[2,1,8,96,1080]{4,3,0,2,1:T(8,128)S(1)} fusion(f32[2,1,8,96,1080]{4,3,0,2,1:T(8,128)} %copy-done, f32[8,1,96,2,96]{2,4,1,3,0:T(8,128)S(1)} %get-tuple-element.44, f32[8,1,96,2,96]{2,4,1,3,0:T(8,128)S(1)} %get-tuple-element.43), kind=kOutput, calls=%fused_computation.48 | convolution fusion | flops 3822354432 | bytes 14450688 | tf_op jit(solution)/shard_map/qsbjr,bpiqj->psbir/dot_general | solution.py:69
  431.7 11.4 %copy.109 = f32[2,1,768,1080]{3,0,1,2:T(2,128)} copy(f32[2,1,768,1080]{3,2,0,1:T(8,128)} %bitcast.263) | data formatting | bytes 13271040 | tf_op jit(solution)/shard_map/reshape | solution.py:103
  454.3 74.0 %all-to-all-done.1 = f32[2,1,768,1080]{3,0,1,2:T(2,128)} async-done(((f32[2,1,768,1080]{3,0,1,2:T(2,128)}), f32[2,1,768,1080]{3,0,1,2:T(2,128)}, u32[]{:S(2)}, u32[]{:S(2)}) %all-to-all-start.1) | async-done | bytes 6635552 | tf_op jit(solution)/shard_map/all_to_all | solution.py:144
  538.8 10.6 %reshape.680 = f32[2,96,96,90,1]{3,2,0,1,4:T(8,128)} reshape(f32[2,1,96,8,1080]{4,3,0,2,1:T(8,128)} %copy.149) | data formatting | bytes 13271040 | tf_op jit(solution)/shard_map/reshape.39
  549.4 13.3 %convolution_bitcast_fusion = f32[2,96,96,90]{2,3,1,0:T(8,128)S(1)} fusion(f32[2,96,96,90,1]{3,2,0,1,4:T(8,128)} %reshape.680, f32[1,90,2,90]{1,3,2,0:T(8,128)S(1)} %copy-done.8, f32[1,90,2,90]{1,3,2,0:T(8,128)S(1)} %copy-done.7), kind=kOutput, calls=%fused_computation.51 | convolution fusion | flops 3583213056 | bytes 13400640 | tf_op jit(solution)/shard_map/psckm,pmqh->qsckh/dot_general | solution.py:148
  562.7 15.4 %fusion.60 = f32[1,96,90,180]{1,3,2,0:T(8,128)S(1)} fusion(f32[2,96,96,90]{2,3,1,0:T(8,128)S(1)} %convolution_bitcast_fusion, f32[1,96,180]{1,2,0:T(8,128)S(1)} %get-tuple-element.54, f32[1,96,180]{1,2,0:T(8,128)S(1)} %get-tuple-element.53), kind=kOutput, calls=%fused_computation.54 | convolution fusion | flops 3583215360 | bytes 12994560 | tf_op jit(solution)/shard_map/qsckh,qkw->schw/dot_general | solution.py:146
  (113 shorter events, 113.4 us)
Async XLA Ops:
  63.6 180.6 %all-to-all-start = ((f32[2,1,96,8640]{2,0,1,3:T(2,128)}), f32[2,1,96,8640]{2,0,1,3:T(2,128)}, u32[]{:S(2)}, u32[]{:S(2)}) async-start(f32[2,1,96,8640]{2,0,1,3:T(2,128)} %bitcast.262), calls=%async_computation | async-start | bytes 17694720 | tf_op jit(solution)/shard_map/all_to_all | solution.py:138
  68.8 310.7 %all-reduce.6.cloned.1.call-start = ((), (), s32[]{:S(2)}) async-start(), calls=%async_computation.4 | async-start | bytes 2383872
  133.7 12.1 %copy-start.4 = (f32[2,8,96,96]{3,2,1,0:T(8,128)S(1)}, f32[2,8,96,96]{3,2,1,0:T(8,128)}, u32[]{:S(2)}) copy-start(f32[2,8,96,96]{3,2,1,0:T(8,128)} %param.8) | copy-start | bytes 1769476
  133.7 12.1 %copy-start.5 = (f32[2,8,96,96]{3,2,1,0:T(8,128)S(1)}, f32[2,8,96,96]{3,2,1,0:T(8,128)}, u32[]{:S(2)}) copy-start(f32[2,8,96,96]{3,2,1,0:T(8,128)} %param.10) | copy-start | bytes 1769476
  141.1 8.6 %copy-start.9 = (f32[2,8,96]{2,1,0:T(8,128)S(1)}, f32[2,8,96]{2,1,0:T(8,128)}, u32[]{:S(2)}) copy-start(f32[2,8,96]{2,1,0:T(8,128)} %param.9) | copy-start | bytes 18436
  141.1 8.6 %copy-start.10 = (f32[2,8,96]{2,1,0:T(8,128)S(1)}, f32[2,8,96]{2,1,0:T(8,128)}, u32[]{:S(2)}) copy-start(f32[2,8,96]{2,1,0:T(8,128)} %param.11) | copy-start | bytes 18436
  141.1 8.7 %collective-permute-start = (f32[2,1,96,1080]{3,2,0,1:T(8,128)}, f32[2,1,96,1080]{3,2,0,1:T(8,128)}, u32[]{:S(2)}, u32[]{:S(2)}) collective-permute-start(f32[2,1,96,1080]{3,2,0,1:T(8,128)} %get-tuple-element.31), channel_id=1, source_target_pairs={{0,1},{1,0},{2,3},{3,2},{4,5},{5,4},{6,7},{7,6},{8,9},{9,8},{10,11... | collective-permute-start | bytes 2488328 | tf_op jit(solution)/shard_map/ppermute | solution.py:26
  141.6 45.5 %collective-permute-start.1 = (f32[2,1,96,1080]{3,2,0,1:T(8,128)}, f32[2,1,96,1080]{3,2,0,1:T(8,128)}, u32[]{:S(2)}, u32[]{:S(2)}) collective-permute-start(f32[2,1,96,1080]{3,2,0,1:T(8,128)} %get-tuple-element.30), channel_id=1, source_target_pairs={{0,2},{1,3},{2,0},{3,1},{4,6},{5,7},{6,4},{7,5},{8,10},{9,11},{10,... | collective-permute-start | bytes 2488328 | tf_op jit(solution)/shard_map/ppermute | solution.py:26
  143.8 60.7 %collective-permute-start.2 = (f32[2,1,96,1080]{3,2,0,1:T(8,128)}, f32[2,1,96,1080]{3,2,0,1:T(8,128)}, u32[]{:S(2)}, u32[]{:S(2)}) collective-permute-start(f32[2,1,96,1080]{3,2,0,1:T(8,128)} %get-tuple-element.29), channel_id=1, source_target_pairs={{0,3},{1,2},{2,1},{3,0},{4,7},{5,6},{6,5},{7,4},{8,11},{9,10},{10,... | collective-permute-start | bytes 2488328 | tf_op jit(solution)/shard_map/ppermute | solution.py:26
  143.9 62.8 %collective-permute-start.3 = (f32[2,1,96,1080]{3,2,0,1:T(8,128)}, f32[2,1,96,1080]{3,2,0,1:T(8,128)}, u32[]{:S(2)}, u32[]{:S(2)}) collective-permute-start(f32[2,1,96,1080]{3,2,0,1:T(8,128)} %get-tuple-element.28), channel_id=1, source_target_pairs={{0,4},{1,5},{2,6},{3,7},{4,0},{5,1},{6,2},{7,3},{8,12},{9,13},{10,... | collective-permute-start | bytes 2488328 | tf_op jit(solution)/shard_map/ppermute | solution.py:26
  145.7 63.1 %collective-permute-start.4 = (f32[2,1,96,1080]{3,2,0,1:T(8,128)}, f32[2,1,96,1080]{3,2,0,1:T(8,128)}, u32[]{:S(2)}, u32[]{:S(2)}) collective-permute-start(f32[2,1,96,1080]{3,2,0,1:T(8,128)} %get-tuple-element.27), channel_id=1, source_target_pairs={{0,5},{1,4},{2,7},{3,6},{4,1},{5,0},{6,3},{7,2},{8,13},{9,12},{10,... | collective-permute-start | bytes 2488328 | tf_op jit(solution)/shard_map/ppermute | solution.py:26
  149.8 76.1 %collective-permute-start.5 = (f32[2,1,96,1080]{3,2,0,1:T(8,128)}, f32[2,1,96,1080]{3,2,0,1:T(8,128)S(1)}, u32[]{:S(2)}, u32[]{:S(2)}) collective-permute-start(f32[2,1,96,1080]{3,2,0,1:T(8,128)} %get-tuple-element.26), channel_id=1, source_target_pairs={{0,6},{1,7},{2,4},{3,5},{4,2},{5,3},{6,0},{7,1},{8,14},{9,15},{10,... | collective-permute-start | bytes 2488328 | tf_op jit(solution)/shard_map/ppermute | solution.py:26
  187.1 56.1 %collective-permute-start.6 = (f32[2,1,96,1080]{3,2,0,1:T(8,128)}, f32[2,1,96,1080]{3,2,0,1:T(8,128)S(1)}, u32[]{:S(2)}, u32[]{:S(2)}) collective-permute-start(f32[2,1,96,1080]{3,2,0,1:T(8,128)} %get-tuple-element.25), channel_id=1, source_target_pairs={{0,7},{1,6},{2,5},{3,4},{4,3},{5,2},{6,1},{7,0},{8,15},{9,14},{10,... | collective-permute-start | bytes 2488328 | tf_op jit(solution)/shard_map/ppermute | solution.py:26
  257.7 9.8 %copy-start.3 = (f32[2,1,768,1080]{3,2,0,1:T(8,128)S(1)}, f32[2,1,768,1080]{3,2,0,1:T(8,128)}, u32[]{:S(2)}) copy-start(f32[2,1,768,1080]{3,2,0,1:T(8,128)} %constant_dynamic-update-slice_fusion) | copy-start | bytes 19906564
  257.7 9.8 %copy-start.6 = (f32[8,1,96,2,96]{2,4,1,3,0:T(8,128)S(1)}, f32[8,1,96,2,96]{2,4,1,3,0:T(8,128)}, u32[]{:S(2)}) copy-start(f32[8,1,96,2,96]{2,4,1,3,0:T(8,128)} %get-tuple-element.42) | copy-start | bytes 1769476
  267.4 28.7 %slice-start = ((s8[7077888]{0:T(1024)(128)(4,1)}), s8[4194304]{0:T(1024)(128)(4,1)S(1)}, s32[]{:S(2)}) async-start(s8[7077888]{0:T(1024)(128)(4,1)} %bitcast.260), calls=%async_computation.5 | async-start | bytes 8388608
  280.6 15.6 %slice-start.1 = ((s8[7077888]{0:T(1024)(128)(4,1)}), s8[2883584]{0:T(1024)(128)(4,1)S(1)}, s32[]{:S(2)}) async-start(s8[7077888]{0:T(1024)(128)(4,1)} %bitcast.260), calls=%async_computation.6 | async-start | bytes 5767168
  296.2 8.7 %copy-start = (f32[2,1,8,96,1080]{4,3,0,2,1:T(8,128)}, f32[2,1,8,96,1080]{4,3,0,2,1:T(8,128)S(1)}, u32[]{:S(2)}) copy-start(f32[2,1,8,96,1080]{4,3,0,2,1:T(8,128)S(1)} %get-tuple-element.63) | copy-start | bytes 19906564
  296.2 8.8 %copy-start.15 = (f32[2,1,8,96,1080]{4,3,0,2,1:T(8,128)S(1)}, f32[2,1,8,96,1080]{4,3,0,2,1:T(8,128)}, u32[]{:S(2)}) copy-start(f32[2,1,8,96,1080]{4,3,0,2,1:T(8,128)} %get-tuple-element.61) | copy-start | bytes 19906564
  321.6 94.8 %all-reduce.4.cloned.1.call-start = ((), (), s32[]{:S(2)}) async-start(), calls=%async_computation.2 | async-start | bytes 303104 | tf_op jit(solution)/shard_map/psum | solution.py:154
  381.2 67.5 %all-gather.3.cloned.1.call-start = ((), (), s32[]{:S(2)}) async-start(), calls=%async_computation.3 | async-start | bytes 1340928 | tf_op jit(solution)/shard_map/all_gather | solution.py:155
  443.1 85.2 %all-to-all-start.1 = ((f32[2,1,768,1080]{3,0,1,2:T(2,128)}), f32[2,1,768,1080]{3,0,1,2:T(2,128)}, u32[]{:S(2)}, u32[]{:S(2)}) async-start(f32[2,1,768,1080]{3,0,1,2:T(2,128)} %copy.109), calls=%async_computation.1 | async-start | bytes 14155776 | tf_op jit(solution)/shard_map/all_to_all | solution.py:144
  538.8 10.6 %copy-start.7 = (f32[1,90,2,90]{1,3,2,0:T(8,128)S(1)}, f32[1,90,2,90]{1,3,2,0:T(8,128)}, u32[]{:S(2)}) copy-start(f32[1,90,2,90]{1,3,2,0:T(8,128)} %get-tuple-element.45) | copy-start | bytes 194404
  538.8 10.6 %copy-start.8 = (f32[1,90,2,90]{1,3,2,0:T(8,128)S(1)}, f32[1,90,2,90]{1,3,2,0:T(8,128)}, u32[]{:S(2)}) copy-start(f32[1,90,2,90]{1,3,2,0:T(8,128)} %get-tuple-element.50) | copy-start | bytes 194404
  (6 other events, 19.4 us)
Sparse Core Ops, SparseCore 0:
  321.7 57.7 all-reduce.5
  382.5 33.8 all-reduce.3
  418.9 24.1 all-gather.2
